TPU v7x, 768 devices: a whole 4x8x12 slice. The times are simulated.
768 devices in a mesh: dp: 192 (over x, z_lo, y, core), pipe: 4 (over z_hi).
Axes of the slice: x: 4, y: 8, z: 12 (z_hi: 4, z_lo: 3; z = z_hi * 3 + z_lo), core: 2. Of those that a mesh axis runs over, the one named last changes fastest.
Arguments:
- stashed: bfloat16 [4, 4, 6144, 8192], P('pipe', None, 'dp'), may hold values from -6 to 6
- kv_grads: bfloat16 [4, 4, 6144, 2048], P('pipe', None, 'dp'), may hold values from -0.0390625 to 0.0390625
- branch_grads: bfloat16 [4, 6144, 8192], P('pipe', 'dp'), may hold values from -6 to 6
- flora_seeds: int32 [4, 2], P('pipe'), may hold values from 0 to 99999
- plan: int32 [4, 4], P('pipe'), may hold values from 0 to 3, each once within a row
Outputs:
- compressed: float32 [4, 256, 2048], P('pipe')
- section_grads: bfloat16 [4, 6144, 8192], P('pipe', 'dp')
Inputs may be any that keep to these rules, and one draw needn't show every extreme that they name: `plan`: each row is a permutation of the micro-batch numbers 0 to 3.
All inputs are finite; a program needn't handle non-finite values.
Results may differ from a plain program's by a relative error of at most 0.0051.
Values may be sent and summed in bfloat16 or wider, within the bound.
A program may use at most 32 MiB of HBM per device.

v0:
```python
import math

import jax
import jax.numpy as jnp
from jax import lax
from jax.sharding import PartitionSpec as P

R = 256


def passed_along(value, axis, steps):
    count = lax.axis_size(axis)
    leading, last = (max(0, -steps), min(count, count - steps))
    return lax.ppermute(value, axis, [(source, source + steps) for source in range(leading, last)])


def projection(seed_value, row_count, col_count):
    row_index = jnp.arange(row_count, dtype=jnp.int32)[:, None]
    col_index = jnp.arange(col_count, dtype=jnp.int32)[None, :]
    hashed_one = (row_index * 1031 + col_index * 2053 + seed_value * 3 + 7) % 32749
    hashed_two = (hashed_one * hashed_one + row_index * 17 + 5) % 32749
    hashed_three = (hashed_two * hashed_two + col_index * 29 + seed_value) % 32749
    scaled = hashed_three.astype(jnp.float32) * (2.0 / 32748.0) - 1.0
    return (scaled * math.sqrt(3.0 / row_count)).astype(jnp.bfloat16)


def contract(left_side, targets):
    return lax.dot_general(
        left_side, targets, (((0,), (0,)), ((), ())), preferred_element_type=jnp.float32
    )


def combine(earlier, later_part):
    return (earlier.astype(jnp.float32) + later_part.astype(jnp.float32)).astype(jnp.bfloat16)


def per_device(stashed, kv_grads, branch_grads, flora_seeds, plan):
    slot_count = stashed.shape[1]
    tokens_dev = stashed.shape[2]
    width_model = stashed.shape[3]
    kv_width = kv_grads.shape[3] // 2
    inputs = stashed[0].reshape(slot_count * tokens_dev, width_model)
    paired = jnp.take(kv_grads[0], plan[0], axis=0).reshape(slot_count * tokens_dev, 2 * kv_width)
    key_proj = projection(flora_seeds[0, 0], width_model, R)
    value_proj = projection(flora_seeds[0, 1], width_model, R)
    stacked_proj = jnp.concatenate([key_proj, value_proj], axis=1)
    projected = jnp.dot(inputs, stacked_proj, preferred_element_type=jnp.float32).astype(
        jnp.bfloat16
    )
    key_total = contract(projected[:, :R], paired[:, :kv_width])
    value_total = contract(projected[:, R:], paired[:, kv_width:])
    key_total, value_total = lax.psum((key_total, value_total), "dp")
    compressed = jnp.concatenate([key_total, value_total], axis=1)[None]
    own_branch = branch_grads[0]
    sections = lax.axis_size("pipe")
    position = lax.axis_index("pipe")
    running = own_branch
    for step_num in range(sections - 1):
        incoming = passed_along(running, "pipe", -1)
        updated = combine(incoming, own_branch)
        running = jnp.where(position == sections - 2 - step_num, updated, running)
    return (compressed, running[None])


def solution(mesh):
    placed = (
        P("pipe", None, "dp", None),
        P("pipe", None, "dp", None),
        P("pipe", "dp", None),
        P("pipe", None),
        P("pipe", None),
    )
    return jax.shard_map(
        per_device,
        mesh=mesh,
        in_specs=placed,
        out_specs=(P("pipe", None, None), P("pipe", "dp", None)),
        check_vma=False,
    )
```

profile of v0, /device:TPU:192, one launch (start us, length us, event | category | flops | bytes accessed | tf_op | source)
XLA Modules:
  0.0 2094.2 jit_solution(11203028557999378606)
XLA Ops:
  7.2 0.0 copy-start
  7.2 0.0 all-reduce.3.cloned.1.call-start
  7.2 8.9 collective-permute-start
  16.1 0.7 fusion.59
  16.8 0.7 compare_and_fusion
  17.4 1.3 fusion.61
  20.1 42.3 %fusion.20 = (bf16[8192,256]{1,0:T(8,128)(2,1)S(1)}, bf16[8192,256]{1,0:T(8,128)(2,1)S(1)}) fusion(s32[]{:T(128)} %bitcast, s32[256]{0:T(256)S(1)} %get-tuple-element.10, s32[8192]{0:T(1024)S(1)} %get-tuple-element.8, s32[]{:T(128)S(6)} %mul.76, s32[256]{0:T(256)S(1)} %get-tuple-element.11, s32[8192]{0:T(1024)S(1)} %get-tuple-element.9, s32[]{:T(128)} %bitcast.1, ...), kind=kLoop, calls=%fused_computation.29 | loop fusion | flops 132120576 | bytes 8456208 | tf_op jit(solution)/shard_map/convert_element_type | solution.py:24
  62.4 0.0 copy-done
  62.4 0.0 copy-start.1
  62.4 2.4 fusion.43
  64.8 0.0 collective-permute-done
  64.8 0.0 copy-done.1
  64.8 1.2 fusion.49
  66.0 0.0 copy-start.2
  66.0 1.9 collective-permute-start.1
  68.0 0.1 broadcast_in_dim.24
  68.0 0.1 broadcast_in_dim.25
  68.1 2.4 gather_fusion
  70.5 1.2 bitcast_select_fusion
  71.7 0.0 copy-done.2
  71.7 42.6 %collective-permute-done.1 = bf16[32,8192]{1,0:T(8,128)(2,1)} collective-permute-done((bf16[32,8192]{1,0:T(8,128)(2,1)S(1)}, bf16[32,8192]{1,0:T(8,128)(2,1)}, u32[]{:S(2)}, u32[]{:S(2)}) %collective-permute-start.1) | collective-permute-done | bytes 524320 | tf_op jit(solution)/shard_map/ppermute | solution.py:14
  114.3 1.2 fusion.52
  115.5 1.9 collective-permute-start.2
  117.5 1.3 fusion.55
  118.7 1.3 fusion.53
  120.0 0.0 all-reduce.3.cloned.1.call-update
  120.0 21.9 %collective-permute-done.2 = bf16[32,8192]{1,0:T(8,128)(2,1)} collective-permute-done((bf16[32,8192]{1,0:T(8,128)(2,1)S(1)}, bf16[32,8192]{1,0:T(8,128)(2,1)}, u32[]{:S(2)}, u32[]{:S(2)}) %collective-permute-start.2) | collective-permute-done | bytes 524320 | tf_op jit(solution)/shard_map/ppermute | solution.py:14
  141.9 2.0 fusion.51
  143.9 1940.4 %all-reduce.3.cloned.1.call-done = (f32[256,1024]{1,0:T(8,128)}, f32[256,1024]{1,0:T(8,128)}) async-done(((f32[256,1024]{1,0:T(8,128)}, f32[256,1024]{1,0:T(8,128)}), (f32[256,1024]{1,0:T(8,128)}, f32[256,1024]{1,0:T(8,128)})) %all-reduce.3.cloned.1.call-update) | async-done | bytes 2097168 | tf_op jit(solution)/shard_map/psum | solution.py:52
  2084.3 3.1 maximum_bitcast_fusion
  (3 shorter events, 0.0 us)
Async XLA Ops:
  7.2 55.2 %copy-start = (bf16[1,4,32,8192]{3,2,1,0:T(8,128)(2,1)S(1)}, bf16[1,4,32,8192]{3,2,1,0:T(8,128)(2,1)}, u32[]{:S(2)}) copy-start(bf16[1,4,32,8192]{3,2,1,0:T(8,128)(2,1)} %param.5) | copy-start | bytes 6291460
  7.2 2077.1 %all-reduce.3.cloned.1.call-start = ((), (), s32[]{:S(2)}) async-start(), calls=%async_computation | async-start | bytes 4194304 | tf_op jit(solution)/shard_map/psum | solution.py:52
  7.2 57.6 %collective-permute-start = (bf16[32,8192]{1,0:T(8,128)(2,1)}, bf16[32,8192]{1,0:T(8,128)(2,1)}, u32[]{:S(2)}, u32[]{:S(2)}) collective-permute-start(bf16[32,8192]{1,0:T(8,128)(2,1)} %bitcast.24), channel_id=1, source_target_pairs={{1,0},{2,1},{3,2},{5,4},{6,5},{7,6},{9,8},{10,9},{11,10},{13,12},{... | collective-permute-start | bytes 1572872 | tf_op jit(solution)/shard_map/ppermute | solution.py:14
  62.4 2.4 copy-start.1
  66.0 5.7 copy-start.2
  66.0 48.3 %collective-permute-start.1 = (bf16[32,8192]{1,0:T(8,128)(2,1)S(1)}, bf16[32,8192]{1,0:T(8,128)(2,1)}, u32[]{:S(2)}, u32[]{:S(2)}) collective-permute-start(bf16[32,8192]{1,0:T(8,128)(2,1)S(1)} %fusion.49), channel_id=1, source_target_pairs={{1,0},{2,1},{3,2},{5,4},{6,5},{7,6},{9,8},{10,9},{11,10},{13,12},{... | collective-permute-start | bytes 1572872 | tf_op jit(solution)/shard_map/ppermute | solution.py:14
  115.5 26.3 %collective-permute-start.2 = (bf16[32,8192]{1,0:T(8,128)(2,1)S(1)}, bf16[32,8192]{1,0:T(8,128)(2,1)}, u32[]{:S(2)}, u32[]{:S(2)}) collective-permute-start(bf16[32,8192]{1,0:T(8,128)(2,1)S(1)} %fusion.52), channel_id=1, source_target_pairs={{1,0},{2,1},{3,2},{5,4},{6,5},{7,6},{9,8},{10,9},{11,10},{13,12},{... | collective-permute-start | bytes 1572872 | tf_op jit(solution)/shard_map/ppermute | solution.py:14
Sparse Core Ops, SparseCore 0:
  120.1 1964.1 all-reduce.2
where the time goes:
time: 2090 us
  waiting for transfers between devices  2000 us (96%)
  other arithmetic  52.3 us (3%)
    psum x1, waiting for transfers between devices, per_device(): key_total, value_total = lax.psum((key_total, value_total), 'dp')  1940 us
    ppermute x3, waiting for transfers between devices, passed_along(): lax.ppermute(value, axis, [(source, source + steps) for source in range(l...  64.4 us
    convert_element_type x1, other arithmetic, projection(): return (scaled * math.sqrt(3.0 / row_count)).astype(jnp.bfloat16)  42.3 us
  transfers between devices with their start and end apart: 4, of which 3 were waited for; matrix products, arithmetic and copies ran while one was open for 3% of the time, Pallas kernels for 0%

commit v1 on v0

v1 whole, which is shorter than its diff:
```python
import math

import jax
import jax.numpy as jnp
from jax import lax
from jax.experimental import pallas as pl
from jax.experimental.pallas import tpu as pltpu
from jax.sharding import PartitionSpec as P

MESH = pl.DeviceIdType.MESH
NX, NZ, NY, SECTIONS = 4, 3, 8, 4
R, D, KVW, MBW, TOK = 256, 8192, 1024, 4, 32
ROWS = MBW * TOK
MOD = 32749
RQ, CQ = R // NX, KVW // NY
Y_ORDER = (4, 3, 5, 2, 6, 1, 7, 0)
KB = 256
STEPS = D // KB
LAG = 4
CHUNKS = 8
CW = D // CHUNKS


def kernel(seeds, plan, x_hbm, kv_hbm, br_hbm, cmp_out, sg_out,
           xo, xp, kvo, kvp, kvg, proj, btab, ctab, acc_o, acc_p, side, tf, tb, xr, qs, qown, yr, zb, fin,
           br, rc, sgs,
           loc_sem, in_send, in_recv, xs_sem, xr_sem, ys_sem, yr_sem, zs_sem, zr_sem,
           gys_sem, gyr_sem, gxs_sem, gxr_sem, ps_sem, pr_sem, cs_sem, cr_sem):
    me = lax.axis_index("dp")
    sec = lax.axis_index("pipe")
    core = me % 2
    y = (me // 2) % NY
    z = (me // (2 * NY)) % NZ
    x = me // (2 * NY * NZ)

    def dp(xx, zz, yy, cc):
        return ((xx * NZ + zz) * NY + yy) * 2 + cc

    partner = (dp(x, z, y, 1 - core), sec)
    x_peer = [(dp((x + d) % NX, z, y, core), sec) for d in range(1, NX)]
    y_peer = [(dp(x, z, (y + off) % NY, core), sec) for off in Y_ORDER[:-1]]
    z_peer = [(dp(x, (z + d) % NZ, y, core), sec) for d in range(1, NZ)]
    below = (me, (sec + SECTIONS - 1) % SECTIONS)
    above = (me, (sec + 1) % SECTIONS)
    peers = [partner, *x_peer, *y_peer, *z_peer, below, above]

    def remote(src, dst, send, recv, device):
        return pltpu.make_async_remote_copy(
            src_ref=src, dst_ref=dst, send_sem=send, recv_sem=recv, device_id=device, device_id_type=MESH
        )

    barrier = pltpu.get_barrier_semaphore()
    for device in peers:
        pl.semaphore_signal(barrier, inc=1, device_id=device, device_id_type=MESH)
    own_cols = pl.ds(pl.multiple_of(core * KVW, KVW), KVW)
    other_cols = pl.ds(pl.multiple_of((1 - core) * KVW, KVW), KVW)
    get_br = pltpu.make_async_copy(br_hbm, br, loc_sem.at[0])
    get_x = pltpu.make_async_copy(x_hbm, xo, loc_sem.at[1])
    get_kv = pltpu.make_async_copy(kv_hbm.at[:, :, own_cols], kvo, loc_sem.at[2])
    get_br.start()
    get_x.start()
    get_kv.start()

    seed = seeds[0, core]
    inv = jnp.float32(1.0 / MOD)
    scale = math.sqrt(3.0 / D)
    slope = jnp.float32(2.0 / 32748.0 * scale)
    low = jnp.float32(-scale)
    high = jnp.float32((2.0 * MOD / 32748.0 - 1.0) * scale)

    def centred(value):
        rest = value - (value.astype(jnp.float32) * inv + 0.5).astype(jnp.int32) * MOD
        return rest

    col = lax.broadcasted_iota(jnp.int32, (R, 128), 0)
    btab[...] = centred(col * 2053)
    ctab[...] = col * 29 + seed

    def make(step):
        for half in range(KB // 128):
            base = pl.multiple_of(step * KB, KB) + half * 128
            row = lax.broadcasted_iota(jnp.int32, (1, 128), 1) + base
            a = centred(row * 1031 + (seed * 3 + 7))
            e = row * 17 + 5
            for g in range(R // 64):
                rows = slice(g * 64, g * 64 + 64)
                one = btab[rows, :] + a
                two = one * one + e
                two = two - (two.astype(jnp.float32) * inv).astype(jnp.int32) * MOD
                three = two * two + ctab[rows, :]
                three = three - (three.astype(jnp.float32) * inv + 0.5).astype(jnp.int32) * MOD
                value = three.astype(jnp.float32) * slope + jnp.where(three < 0, high, low)
                proj[rows, pl.ds(base, 128)] = value.astype(jnp.bfloat16)

    def multiply(step, inputs, acc):
        cols = pl.ds(pl.multiple_of(step * KB, KB), KB)
        acc[...] += lax.dot_general(
            proj[:, cols], inputs[:, cols], (((1,), (1,)), ((), ())), preferred_element_type=jnp.float32
        )

    acc_o[...] = jnp.zeros_like(acc_o)
    acc_p[...] = jnp.zeros_like(acc_p)

    @pl.loop(0, LAG)
    def _(step):
        make(step)

    pl.semaphore_wait(barrier, len(peers))
    halves = [pl.ds(h * (D // 2), D // 2) for h in range(2)]
    give = [remote(x_hbm.at[:, halves[h]], xp.at[:, halves[h]], in_send.at[h], in_recv.at[h], partner) for h in range(2)]
    give.append(remote(kv_hbm.at[:, :, other_cols], kvp, in_send.at[2], in_recv.at[2], partner))
    for copy in give:
        copy.start()
    get_br.wait()

    def chunk(k):
        return pl.ds(pl.multiple_of(k * CW, CW), CW)

    def relay(source, k):
        return remote(source.at[:, chunk(k)], rc.at[:, chunk(k)], cs_sem.at[k], cr_sem.at[k], below)

    @pl.when(sec == SECTIONS - 1)
    def _():
        for k in range(CHUNKS):
            relay(br, k).start()
        sg_out[...] = br[...]

    def chain(point):
        k = point - 2 * (SECTIONS - 2 - sec)

        @pl.when((sec < SECTIONS - 1) & (k >= 0) & (k < CHUNKS))
        def _():
            relay(br, k).wait_recv()
            cols = chunk(k)
            total = (rc[:, cols].astype(jnp.float32) + br[:, cols].astype(jnp.float32)).astype(jnp.bfloat16)
            sgs[:, cols] = total
            sg_out[:, cols] = total

            @pl.when(sec > 0)
            def _():
                relay(sgs, k).start()

    get_x.wait()

    @pl.loop(LAG, STEPS // 2)
    def _(step):
        make(step)
        multiply(step - LAG, xo, acc_o)

    give[0].wait_recv()

    @pl.loop(STEPS // 2, STEPS)
    def _(step):
        make(step)
        multiply(step - LAG, xo, acc_o)
        multiply(step - STEPS // 2, xp, acc_p)

    @pl.loop(STEPS - LAG, STEPS)
    def _(step):
        multiply(step, xo, acc_o)

    give[1].wait_recv()

    @pl.loop(STEPS // 2, STEPS)
    def _(step):
        multiply(step, xp, acc_p)

    side[:, :ROWS] = acc_o[...].astype(jnp.bfloat16)
    side[:, ROWS:] = acc_p[...].astype(jnp.bfloat16)
    get_kv.wait()
    give[2].wait_recv()
    for slot in range(MBW):
        batch = plan[0, slot]
        kvg[slot * TOK:(slot + 1) * TOK, :] = kvo[batch]
        kvg[ROWS + slot * TOK:ROWS + (slot + 1) * TOK, :] = kvp[batch]
    chain(0)

    copies = []

    def start(copy):
        copy.start()
        copies.append(copy)
        return copy

    blocks = [(y + off) % NY for off in Y_ORDER]
    x_copy = {}

    def send_x(j):
        for d in range(1, NX):
            x_copy[d, j] = start(
                remote(tb.at[(x + d) % NX, j], xr.at[d - 1, j], xs_sem.at[d - 1, j], xr_sem.at[d - 1, j], x_peer[d - 1])
            )

    for j in range(NY):
        cols = pl.ds(pl.multiple_of(blocks[j] * CQ, CQ), CQ)
        part = jnp.dot(side[...], kvg[:, cols], preferred_element_type=jnp.float32)
        for q in range(NX):
            piece = part[q * RQ:(q + 1) * RQ, :]
            tf[q, j] = piece
            tb[q, j] = piece.astype(jnp.bfloat16)
        if j:
            send_x(j - 1)
    send_x(NY - 1)
    chain(1)

    y_copy = []
    for j in range(NY):
        total = tf[x, j]
        for d in range(1, NX):
            x_copy[d, j].wait_recv()
            total = total + xr[d - 1, j].astype(jnp.float32)
        if j < NY - 1:
            qs[j] = total.astype(jnp.bfloat16)
            y_copy.append(start(remote(qs.at[j], yr.at[j], ys_sem.at[j], yr_sem.at[j], y_peer[j])))
        else:
            qown[...] = total
        if j in (1, 4):
            chain(2 if j == 1 else 3)

    chain(4)
    total = qown[...]
    for j in range(NY - 1):
        y_copy[j].wait_recv()
        total = total + yr[j].astype(jnp.float32)
    zb[z] = total.astype(jnp.bfloat16)
    z_copy = [
        start(remote(zb.at[z], zb.at[z], zs_sem.at[d], zr_sem.at[d], z_peer[d])) for d in range(NZ - 1)
    ]
    chain(5)
    for copy in z_copy:
        copy.wait_recv()
    total = (zb[0].astype(jnp.float32) + zb[1].astype(jnp.float32)) + zb[2].astype(jnp.float32)
    fin[core, x, y] = total.astype(jnp.bfloat16)

    mine = fin.at[core, x, y]
    gy_copy = [start(remote(mine, mine, gys_sem.at[j], gyr_sem.at[j], y_peer[j])) for j in range(NY - 1)]
    gx_copy = {}

    def to_partner(xx, yy):
        piece = fin.at[core, xx, yy]
        remote(piece, piece, ps_sem, pr_sem, partner).start()

    for j in range(NY - 1, -1, -1):
        yy = (y - Y_ORDER[j]) % NY
        if j < NY - 1:
            gy_copy[j].wait_recv()
        piece = fin.at[core, x, yy]
        for d in range(1, NX):
            gx_copy[d, j] = start(remote(piece, piece, gxs_sem.at[d - 1, j], gxr_sem.at[d - 1, j], x_peer[d - 1]))
        to_partner(x, yy)
        if j in (6, 3):
            chain(6 if j == 6 else 7)
    chain(8)
    for j in range(NY - 1, -1, -1):
        yy = (y - Y_ORDER[j]) % NY
        for d in range(1, NX):
            gx_copy[d, j].wait_recv()
            to_partner((x + NX - d) % NX, yy)
        if j in (5, 2):
            chain(9 if j == 5 else 10)
    chain(11)
    whole = remote(fin.at[core], fin.at[core], ps_sem, pr_sem, partner)
    whole.wait_recv()
    for role in range(2):
        for q in range(NX):
            for b in range(NY):
                cmp_out[q * RQ:(q + 1) * RQ, role * KVW + b * CQ:role * KVW + (b + 1) * CQ] = fin[role, q, b]
    whole.wait_send()
    for copy in copies + give:
        copy.wait_send()

    @pl.when(sec > 0)
    def _():
        for k in range(CHUNKS):
            relay(br, k).wait_send()


def per_device(stashed, kv_grads, branch_grads, flora_seeds, plan):
    vmem = pltpu.VMEM
    bf16, f32, i32 = jnp.bfloat16, jnp.float32, jnp.int32
    dma = pltpu.SemaphoreType.DMA
    compressed, grads = pl.pallas_call(
        kernel,
        out_shape=(jax.ShapeDtypeStruct((R, 2 * KVW), bf16), jax.ShapeDtypeStruct((TOK, D), bf16)),
        in_specs=[pl.BlockSpec(memory_space=pltpu.SMEM)] * 2 + [pl.BlockSpec(memory_space=pl.ANY)] * 3,
        out_specs=(pl.BlockSpec(memory_space=vmem), pl.BlockSpec(memory_space=vmem)),
        scratch_shapes=[
            vmem((ROWS, D), bf16), vmem((ROWS, D), bf16),
            vmem((MBW, TOK, KVW), bf16), vmem((MBW, TOK, KVW), bf16), vmem((2 * ROWS, KVW), bf16),
            vmem((R, D), bf16), vmem((R, 128), i32), vmem((R, 128), i32),
            vmem((R, ROWS), f32), vmem((R, ROWS), f32), vmem((R, 2 * ROWS), bf16),
            vmem((NX, NY, RQ, CQ), f32), vmem((NX, NY, RQ, CQ), bf16), vmem((NX - 1, NY, RQ, CQ), bf16),
            vmem((NY - 1, RQ, CQ), bf16), vmem((RQ, CQ), f32), vmem((NY - 1, RQ, CQ), bf16),
            vmem((NZ, RQ, CQ), bf16), vmem((2, NX, NY, RQ, CQ), bf16),
            vmem((TOK, D), bf16), vmem((TOK, D), bf16), vmem((TOK, D), bf16),
            dma((3,)), dma((3,)), dma((3,)),
            dma((NX - 1, NY)), dma((NX - 1, NY)), dma((NY - 1,)), dma((NY - 1,)), dma((NZ - 1,)), dma((NZ - 1,)),
            dma((NY - 1,)), dma((NY - 1,)), dma((NX - 1, NY)), dma((NX - 1, NY)), dma, dma,
            dma((CHUNKS,)), dma((CHUNKS,)),
        ],
        compiler_params=pltpu.CompilerParams(
            collective_id=0, has_side_effects=True, vmem_limit_bytes=60 * 1024 * 1024
        ),
    )(flora_seeds, plan, stashed.reshape(ROWS, D), kv_grads.reshape(MBW, TOK, 2 * KVW), branch_grads.reshape(TOK, D))
    return compressed.astype(f32)[None], grads[None]


def solution(mesh):
    placed = (
        P("pipe", None, "dp", None),
        P("pipe", None, "dp", None),
        P("pipe", "dp", None),
        P("pipe", None),
        P("pipe", None),
    )
    return jax.shard_map(
        per_device,
        mesh=mesh,
        in_specs=placed,
        out_specs=(P("pipe", None, None), P("pipe", "dp", None)),
        check_vma=False,
    )
```

time: 2090 us -> 98 us (0.05)
  the two profiles are of different devices: /device:TPU:192 before, /device:TPU:1 now
where the time goes in v1:
time: 98 us; the launch traced here: 97.8 us
  Pallas kernels  93.5 us (95%)
  other arithmetic  2.85 us (3%)
    pallas_call x1, Pallas kernels, per_device(): pl.pallas_call(kernel, out_shape=(jax.ShapeDtypeStruct((R, 2 * KVW), bf16...  93.5 us
    broadcast_in_dim x1, other arithmetic, per_device(): return (compressed.astype(f32)[None], grads[None])  2.85 us

profile of v1, /device:TPU:1, one launch (start us, length us, event | category | flops | bytes accessed | tf_op | source)
XLA Modules:
  0.0 97.8 jit_solution(2064085593795131036)
XLA Ops:
  0.6 93.5 %shard_map.68 = (bf16[256,2048]{1,0:T(8,128)(2,1)}, bf16[32,8192]{1,0:T(8,128)(2,1)}) custom-call(s32[1,2]{1,0:T(1,128)} %seeds.1, s32[1,4]{1,0:T(1,128)} %plan.1, bf16[128,8192]{1,0:T(8,128)(2,1)} %bitcast.7, bf16[4,32,2048]{2,1,0:T(8,128)(2,1)} %bitcast.9, bf16[32,8192]{1,0:T(8,128)(2,1)} %bitcast.10), custom_call_target="tpu_custom_call" | custom-call | tf_op jit(solution)/shard_map/pallas_call | solution.py:282
  94.2 0.0 copy-start
  94.2 2.8 %bitcast_convert_fusion = f32[1,256,2048]{2,1,0:T(8,128)} fusion(bf16[256,2048]{1,0:T(8,128)(2,1)} %get-tuple-element.4), kind=kLoop, calls=%fused_computation | loop fusion | flops 524288 | bytes 3145728 | tf_op jit(solution)/shard_map/broadcast_in_dim | solution.py:305
  97.0 0.0 copy-done
  97.0 0.8 copy.8
Async XLA Ops:
  94.2 2.9 %copy-start = (bf16[32,8192]{1,0:T(8,128)(2,1)S(1)}, bf16[32,8192]{1,0:T(8,128)(2,1)}, u32[]{:S(2)}) copy-start(bf16[32,8192]{1,0:T(8,128)(2,1)} %get-tuple-element.5) | copy-start | bytes 1572868

commit v2 on v1

--- a/solution.py
+++ b/solution.py
@@ -14,16 +14,18 @@
 MOD = 32749
 RQ, CQ = R // NX, KVW // NY
 Y_ORDER = (4, 3, 5, 2, 6, 1, 7, 0)
-KB = 256
+KB = 512
 STEPS = D // KB
-LAG = 4
-CHUNKS = 8
+LAG = 2
+TAIL = 1024
+CHUNKS = 16
 CW = D // CHUNKS
+WINDOW = 4
 
 
 def kernel(seeds, plan, x_hbm, kv_hbm, br_hbm, cmp_out, sg_out,
            xo, xp, kvo, kvp, kvg, proj, btab, ctab, acc_o, acc_p, side, tf, tb, xr, qs, qown, yr, zb, fin,
-           br, rc, sgs,
+           br, rc, sgs, above_sum, br_sem, rs_sem, rr_sem,
            loc_sem, in_send, in_recv, xs_sem, xr_sem, ys_sem, yr_sem, zs_sem, zr_sem,
            gys_sem, gyr_sem, gxs_sem, gxr_sem, ps_sem, pr_sem, cs_sem, cr_sem):
     me = lax.axis_index("dp")
@@ -52,12 +54,16 @@
     barrier = pltpu.get_barrier_semaphore()
     for device in peers:
         pl.semaphore_signal(barrier, inc=1, device_id=device, device_id_type=MESH)
+
     own_cols = pl.ds(pl.multiple_of(core * KVW, KVW), KVW)
     other_cols = pl.ds(pl.multiple_of((1 - core) * KVW, KVW), KVW)
-    get_br = pltpu.make_async_copy(br_hbm, br, loc_sem.at[0])
+    get_br = [
+        pltpu.make_async_copy(br_hbm.at[:, k * CW:(k + 1) * CW], br.at[k], br_sem.at[k]) for k in range(CHUNKS)
+    ]
     get_x = pltpu.make_async_copy(x_hbm, xo, loc_sem.at[1])
     get_kv = pltpu.make_async_copy(kv_hbm.at[:, :, own_cols], kvo, loc_sem.at[2])
-    get_br.start()
+    for copy in get_br:
+        copy.start()
     get_x.start()
     get_kv.start()
 
@@ -66,7 +72,7 @@
     scale = math.sqrt(3.0 / D)
     slope = jnp.float32(2.0 / 32748.0 * scale)
     low = jnp.float32(-scale)
-    high = jnp.float32((2.0 * MOD / 32748.0 - 1.0) * scale)
+    inv_up = jnp.float32((1.0 + 5e-7) / MOD)
 
     def centred(value):
         rest = value - (value.astype(jnp.float32) * inv + 0.5).astype(jnp.int32) * MOD
@@ -88,12 +94,13 @@
                 two = one * one + e
                 two = two - (two.astype(jnp.float32) * inv).astype(jnp.int32) * MOD
                 three = two * two + ctab[rows, :]
-                three = three - (three.astype(jnp.float32) * inv + 0.5).astype(jnp.int32) * MOD
-                value = three.astype(jnp.float32) * slope + jnp.where(three < 0, high, low)
+                rest = (three - (three >> 15) * MOD).astype(jnp.float32)
+                rest = rest - jnp.floor(rest * inv_up) * jnp.float32(MOD)
+                value = rest * slope + low
                 proj[rows, pl.ds(base, 128)] = value.astype(jnp.bfloat16)
 
-    def multiply(step, inputs, acc):
-        cols = pl.ds(pl.multiple_of(step * KB, KB), KB)
+    def multiply(step, width, inputs, acc):
+        cols = pl.ds(pl.multiple_of(step * width, width), width)
         acc[...] += lax.dot_general(
             proj[:, cols], inputs[:, cols], (((1,), (1,)), ((), ())), preferred_element_type=jnp.float32
         )
@@ -111,60 +118,65 @@
     give.append(remote(kv_hbm.at[:, :, other_cols], kvp, in_send.at[2], in_recv.at[2], partner))
     for copy in give:
         copy.start()
-    get_br.wait()
-
-    def chunk(k):
-        return pl.ds(pl.multiple_of(k * CW, CW), CW)
-
-    def relay(source, k):
-        return remote(source.at[:, chunk(k)], rc.at[:, chunk(k)], cs_sem.at[k], cr_sem.at[k], below)
+    for copy in get_br:
+        copy.wait()
+
+    def raw(k):
+        return remote(br.at[k], rc.at[k], cs_sem.at[k], cr_sem.at[k], (me, sec + 1 - 2 * (sec % 2)))
+
+    def relay(k):
+        return remote(sgs.at[k], above_sum.at[k], rs_sem.at[k], rr_sem.at[k], (me, SECTIONS - 1 - sec))
+
+    def added(first, second):
+        return (first.astype(jnp.float32) + second.astype(jnp.float32)).astype(jnp.bfloat16)
+
+    @pl.when(sec >= 2)
+    def _():
+        for k in range(WINDOW):
+            raw(k).start()
+
+    @pl.when(sec == 1)
+    def _():
+        for k in range(CHUNKS):
+            raw(k).start()
 
     @pl.when(sec == SECTIONS - 1)
     def _():
         for k in range(CHUNKS):
-            relay(br, k).start()
-        sg_out[...] = br[...]
-
-    def chain(point):
-        k = point - 2 * (SECTIONS - 2 - sec)
-
-        @pl.when((sec < SECTIONS - 1) & (k >= 0) & (k < CHUNKS))
+            sg_out[:, k * CW:(k + 1) * CW] = br[k]
+
+    def chain(k):
+        @pl.when(sec >= 2)
         def _():
-            relay(br, k).wait_recv()
-            cols = chunk(k)
-            total = (rc[:, cols].astype(jnp.float32) + br[:, cols].astype(jnp.float32)).astype(jnp.bfloat16)
-            sgs[:, cols] = total
-            sg_out[:, cols] = total
-
-            @pl.when(sec > 0)
+            raw(k).wait_recv()
+            total = added(rc[k], br[k])
+            sgs[k] = total
+
+            @pl.when(sec == 2)
             def _():
-                relay(sgs, k).start()
+                sg_out[:, k * CW:(k + 1) * CW] = total
+
+            if k + WINDOW < CHUNKS:
+                raw(k + WINDOW).start()
+            relay(k).start()
 
     get_x.wait()
 
-    @pl.loop(LAG, STEPS // 2)
+    @pl.loop(LAG, STEPS)
     def _(step):
         make(step)
-        multiply(step - LAG, xo, acc_o)
-
-    give[0].wait_recv()
-
-    @pl.loop(STEPS // 2, STEPS)
+        multiply(step - LAG, KB, xo, acc_o)
+
+    chain(0)
+    multiply(D // TAIL - 1, TAIL, xo, acc_o)
+    for copy in give[:2]:
+        copy.wait_recv()
+
+    @pl.loop(0, D // TAIL)
     def _(step):
-        make(step)
-        multiply(step - LAG, xo, acc_o)
-        multiply(step - STEPS // 2, xp, acc_p)
-
-    @pl.loop(STEPS - LAG, STEPS)
-    def _(step):
-        multiply(step, xo, acc_o)
-
-    give[1].wait_recv()
-
-    @pl.loop(STEPS // 2, STEPS)
-    def _(step):
-        multiply(step, xp, acc_p)
-
+        multiply(step, TAIL, xp, acc_p)
+
+    chain(1)
     side[:, :ROWS] = acc_o[...].astype(jnp.bfloat16)
     side[:, ROWS:] = acc_p[...].astype(jnp.bfloat16)
     get_kv.wait()
@@ -173,7 +185,6 @@
         batch = plan[0, slot]
         kvg[slot * TOK:(slot + 1) * TOK, :] = kvo[batch]
         kvg[ROWS + slot * TOK:ROWS + (slot + 1) * TOK, :] = kvp[batch]
-    chain(0)
 
     copies = []
 
@@ -201,7 +212,7 @@
         if j:
             send_x(j - 1)
     send_x(NY - 1)
-    chain(1)
+    chain(2)
 
     y_copy = []
     for j in range(NY):
@@ -214,19 +225,20 @@
             y_copy.append(start(remote(qs.at[j], yr.at[j], ys_sem.at[j], yr_sem.at[j], y_peer[j])))
         else:
             qown[...] = total
-        if j in (1, 4):
-            chain(2 if j == 1 else 3)
-
-    chain(4)
+        if j % 2:
+            chain(3 + j // 2)
+
     total = qown[...]
     for j in range(NY - 1):
         y_copy[j].wait_recv()
         total = total + yr[j].astype(jnp.float32)
+        if j in (2, 5):
+            chain(7 + j // 3)
     zb[z] = total.astype(jnp.bfloat16)
     z_copy = [
         start(remote(zb.at[z], zb.at[z], zs_sem.at[d], zr_sem.at[d], z_peer[d])) for d in range(NZ - 1)
     ]
-    chain(5)
+    chain(9)
     for copy in z_copy:
         copy.wait_recv()
     total = (zb[0].astype(jnp.float32) + zb[1].astype(jnp.float32)) + zb[2].astype(jnp.float32)
@@ -248,17 +260,33 @@
         for d in range(1, NX):
             gx_copy[d, j] = start(remote(piece, piece, gxs_sem.at[d - 1, j], gxr_sem.at[d - 1, j], x_peer[d - 1]))
         to_partner(x, yy)
-        if j in (6, 3):
-            chain(6 if j == 6 else 7)
-    chain(8)
+        if j in (5, 3, 1):
+            chain(10 + (5 - j) // 2)
+    chain(13)
     for j in range(NY - 1, -1, -1):
         yy = (y - Y_ORDER[j]) % NY
         for d in range(1, NX):
             gx_copy[d, j].wait_recv()
             to_partner((x + NX - d) % NX, yy)
-        if j in (5, 2):
-            chain(9 if j == 5 else 10)
-    chain(11)
+        if j in (5, 3):
+            chain(14 + (5 - j) // 2)
+
+    @pl.when(sec < 2)
+    def _():
+        @pl.loop(0, CHUNKS)
+        def _(k):
+            cols = pl.ds(pl.multiple_of(k * CW, CW), CW)
+            relay(k).wait_recv()
+
+            @pl.when(sec == 1)
+            def _():
+                sg_out[:, cols] = added(above_sum[k], br[k])
+
+            @pl.when(sec == 0)
+            def _():
+                raw(k).wait_recv()
+                sg_out[:, cols] = added(added(above_sum[k], rc[k]), br[k])
+
     whole = remote(fin.at[core], fin.at[core], ps_sem, pr_sem, partner)
     whole.wait_recv()
     for role in range(2):
@@ -272,7 +300,12 @@
     @pl.when(sec > 0)
     def _():
         for k in range(CHUNKS):
-            relay(br, k).wait_send()
+            raw(k).wait_send()
+
+    @pl.when(sec >= 2)
+    def _():
+        for k in range(CHUNKS):
+            relay(k).wait_send()
 
 
 def per_device(stashed, kv_grads, branch_grads, flora_seeds, plan):
@@ -292,7 +325,8 @@
             vmem((NX, NY, RQ, CQ), f32), vmem((NX, NY, RQ, CQ), bf16), vmem((NX - 1, NY, RQ, CQ), bf16),
             vmem((NY - 1, RQ, CQ), bf16), vmem((RQ, CQ), f32), vmem((NY - 1, RQ, CQ), bf16),
             vmem((NZ, RQ, CQ), bf16), vmem((2, NX, NY, RQ, CQ), bf16),
-            vmem((TOK, D), bf16), vmem((TOK, D), bf16), vmem((TOK, D), bf16),
+            vmem((CHUNKS, TOK, CW), bf16), vmem((CHUNKS, TOK, CW), bf16), vmem((CHUNKS, TOK, CW), bf16),
+            vmem((CHUNKS, TOK, CW), bf16), dma((CHUNKS,)), dma((CHUNKS,)), dma((CHUNKS,)),
             dma((3,)), dma((3,)), dma((3,)),
             dma((NX - 1, NY)), dma((NX - 1, NY)), dma((NY - 1,)), dma((NY - 1,)), dma((NZ - 1,)), dma((NZ - 1,)),
             dma((NY - 1,)), dma((NY - 1,)), dma((NX - 1, NY)), dma((NX - 1, NY)), dma, dma,

time: 98 us -> 73.7 us (0.75)
  Pallas kernels: 93.5 us -> 68.5 us
    pallas_call x1, Pallas kernels: 93.5 us -> 68.5 us  [per_device(): pl.pallas_call(kernel, out_shape=(jax.ShapeDtypeStruct((R, 2 * KVW), bf16...]
where the time goes in v2:
time: 73.7 us; the launch traced here: 72.8 us
  Pallas kernels  68.5 us (93%)
  other arithmetic  2.85 us (4%)
  local copies, waits for them, and re-layouts  0.8 us (1%)
    pallas_call x1, Pallas kernels, per_device(): pl.pallas_call(kernel, out_shape=(jax.ShapeDtypeStruct((R, 2 * KVW), bf16...  68.5 us
    broadcast_in_dim x1, other arithmetic, per_device(): return (compressed.astype(f32)[None], grads[None])  2.85 us

profile of v2, /device:TPU:1, one launch (start us, length us, event | category | flops | bytes accessed | tf_op | source)
XLA Modules:
  0.0 72.8 jit_solution(8092151917641768435)
XLA Ops:
  0.6 68.5 %shard_map.68 = (bf16[256,2048]{1,0:T(8,128)(2,1)}, bf16[32,8192]{1,0:T(8,128)(2,1)}) custom-call(s32[1,2]{1,0:T(1,128)} %seeds.1, s32[1,4]{1,0:T(1,128)} %plan.1, bf16[128,8192]{1,0:T(8,128)(2,1)} %bitcast.7, bf16[4,32,2048]{2,1,0:T(8,128)(2,1)} %bitcast.9, bf16[32,8192]{1,0:T(8,128)(2,1)} %bitcast.10), custom_call_target="tpu_custom_call" | custom-call | tf_op jit(solution)/shard_map/pallas_call | solution.py:315
  69.1 0.0 copy-start
  69.1 2.8 %bitcast_convert_fusion = f32[1,256,2048]{2,1,0:T(8,128)} fusion(bf16[256,2048]{1,0:T(8,128)(2,1)} %get-tuple-element.4), kind=kLoop, calls=%fused_computation | loop fusion | flops 524288 | bytes 3145728 | tf_op jit(solution)/shard_map/broadcast_in_dim | solution.py:339
  72.0 0.0 copy-done
  72.0 0.8 %copy.8 = bf16[1,32,8192]{2,1,0:T(8,128)(2,1)} copy(bf16[1,32,8192]{2,1,0:T(8,128)(2,1)S(1)} %bitcast.8) | data formatting | bytes 1048576
Async XLA Ops:
  69.1 2.9 %copy-start = (bf16[32,8192]{1,0:T(8,128)(2,1)S(1)}, bf16[32,8192]{1,0:T(8,128)(2,1)}, u32[]{:S(2)}) copy-start(bf16[32,8192]{1,0:T(8,128)(2,1)} %get-tuple-element.5) | copy-start | bytes 1572868

commit v3 on v2

--- a/solution.py
+++ b/solution.py
@@ -20,6 +20,7 @@
 TAIL = 1024
 CHUNKS = 16
 CW = D // CHUNKS
+AHEAD = 4
 WINDOW = 4
 
 
@@ -137,8 +138,7 @@
 
     @pl.when(sec == 1)
     def _():
-        for k in range(CHUNKS):
-            raw(k).start()
+        raw(0).start()
 
     @pl.when(sec == SECTIONS - 1)
     def _():
@@ -146,6 +146,11 @@
             sg_out[:, k * CW:(k + 1) * CW] = br[k]
 
     def chain(k):
+        if k + 1 < CHUNKS:
+            @pl.when(sec == 1)
+            def _():
+                raw(k + 1).start()
+
         @pl.when(sec >= 2)
         def _():
             raw(k).wait_recv()
@@ -209,9 +214,8 @@
             piece = part[q * RQ:(q + 1) * RQ, :]
             tf[q, j] = piece
             tb[q, j] = piece.astype(jnp.bfloat16)
-        if j:
+        if 0 < j <= AHEAD:
             send_x(j - 1)
-    send_x(NY - 1)
     chain(2)
 
     y_copy = []
@@ -220,6 +224,8 @@
         for d in range(1, NX):
             x_copy[d, j].wait_recv()
             total = total + xr[d - 1, j].astype(jnp.float32)
+        if j + AHEAD < NY:
+            send_x(j + AHEAD)
         if j < NY - 1:
             qs[j] = total.astype(jnp.bfloat16)
             y_copy.append(start(remote(qs.at[j], yr.at[j], ys_sem.at[j], yr_sem.at[j], y_peer[j])))

time: 73.7 us -> 72.5 us (0.984)
  the two profiles are of different devices: /device:TPU:1 before, /device:TPU:131 now
where the time goes in v3:
time: 72.5 us; the launch traced here: 72.3 us
  Pallas kernels  68 us (94%)
  other arithmetic  2.85 us (4%)
  local copies, waits for them, and re-layouts  0.8 us (1%)
    pallas_call x1, Pallas kernels, per_device(): pl.pallas_call(kernel, out_shape=(jax.ShapeDtypeStruct((R, 2 * KVW), bf16...  68 us
    broadcast_in_dim x1, other arithmetic, per_device(): return (compressed.astype(f32)[None], grads[None])  2.85 us

profile of v3, /device:TPU:131, one launch (start us, length us, event | category | flops | bytes accessed | tf_op | source)
XLA Modules:
  0.0 72.3 jit_solution(5075961208076219592)
XLA Ops:
  0.6 68.0 %shard_map.68 = (bf16[256,2048]{1,0:T(8,128)(2,1)}, bf16[32,8192]{1,0:T(8,128)(2,1)}) custom-call(s32[1,2]{1,0:T(1,128)} %seeds.1, s32[1,4]{1,0:T(1,128)} %plan.1, bf16[128,8192]{1,0:T(8,128)(2,1)} %bitcast.7, bf16[4,32,2048]{2,1,0:T(8,128)(2,1)} %bitcast.9, bf16[32,8192]{1,0:T(8,128)(2,1)} %bitcast.10), custom_call_target="tpu_custom_call" | custom-call | tf_op jit(solution)/shard_map/pallas_call | solution.py:321
  68.6 0.0 copy-start
  68.6 2.8 %bitcast_convert_fusion = f32[1,256,2048]{2,1,0:T(8,128)} fusion(bf16[256,2048]{1,0:T(8,128)(2,1)} %get-tuple-element.4), kind=kLoop, calls=%fused_computation | loop fusion | flops 524288 | bytes 3145728 | tf_op jit(solution)/shard_map/broadcast_in_dim | solution.py:345
  71.5 0.0 copy-done
  71.5 0.8 %copy.8 = bf16[1,32,8192]{2,1,0:T(8,128)(2,1)} copy(bf16[1,32,8192]{2,1,0:T(8,128)(2,1)S(1)} %bitcast.8) | data formatting | bytes 1048576
Async XLA Ops:
  68.6 2.9 %copy-start = (bf16[32,8192]{1,0:T(8,128)(2,1)S(1)}, bf16[32,8192]{1,0:T(8,128)(2,1)}, u32[]{:S(2)}) copy-start(bf16[32,8192]{1,0:T(8,128)(2,1)} %get-tuple-element.5) | copy-start | bytes 1572868
